TPU v7x, 256 devices: a whole 4x4x8 slice. The times are simulated.
256 devices in a mesh: pp: 8 (over z_lo, y), ep: 32 (over x, z_hi, core).
Axes of the slice: x: 4, y: 4, z: 8 (z_hi: 4, z_lo: 2; z = z_hi * 2 + z_lo), core: 2. Of those that a mesh axis runs over, the one named last changes fastest.
Arguments:
- fwd_tokens: bfloat16 [8, 4096, 4096], P('pp', 'ep'), may hold values from -6 to 6
- fwd_routes: int32 [8, 4096, 1], P('pp', 'ep'), may hold values from 0 to 7; in each aligned block of 128 rows (0 to 127, 128 to 255, ..., all dimensions but the last counted through in order) at most 24 rows name the same one
- fwd_gates: float32 [8, 4096, 1], P('pp', 'ep'), may hold values from 0.05 to 0.6
- bwd_tokens: bfloat16 [8, 4096, 4096], P('pp', 'ep'), may hold values from -6 to 6
- bwd_grads: bfloat16 [8, 4096, 4096], P('pp', 'ep'), may hold values from -6 to 6
- bwd_routes: int32 [8, 4096, 1], P('pp', 'ep'), may hold values from 0 to 7; in each aligned block of 128 rows (0 to 127, 128 to 255, ..., all dimensions but the last counted through in order) at most 24 rows name the same one
- bwd_gates: float32 [8, 4096, 1], P('pp', 'ep'), may hold values from 0.05 to 0.6
- gate_proj: bfloat16 [8, 32, 1024, 768], P('pp', 'ep'), may hold values from -0.09375 to 0.09375
- up_proj: bfloat16 [8, 32, 1024, 768], P('pp', 'ep'), may hold values from -0.09375 to 0.09375
- down_proj: bfloat16 [8, 32, 768, 1024], P('pp', 'ep'), may hold values from -0.21875 to 0.21875
Outputs:
- handed_forward: bfloat16 [8, 4096, 4096], P('pp', 'ep')
- handed_backward: bfloat16 [8, 4096, 4096], P('pp', 'ep')
Inputs may be any that keep to these rules, and one draw needn't show every extreme that they name: `fwd_routes`: among the 128 tokens of one index of ep, no expert is named by more than 24 tokens, and in some such block an expert is named exactly 24 times. `bwd_routes`: among the 128 tokens of one index of ep, no expert is named by more than 24 tokens, and in some such block an expert is named exactly 24 times.
All inputs are finite; a program needn't handle non-finite values.
Results may differ from a plain program's by a relative error of at most 0.0071.
Values may be sent and summed in bfloat16 or wider, within the bound.
A program may use at most 128 MiB of HBM per device.

v0:
```python
import jax
import jax.numpy as jnp
from jax import lax
from jax.sharding import PartitionSpec as P


def partner(block, axis, distance):
    count = lax.axis_size(axis)
    route = []
    for low in range(count):
        high = low | 1 << distance
        if high != low and high < count:
            route += [(low, high), (high, low)]
    return lax.ppermute(block, axis, route)


def shifted(shard, axis, by):
    count = lax.axis_size(axis)
    pairs = [(i, i + by) for i in range(count) if 0 <= i + by < count]
    return lax.ppermute(shard, axis, pairs)


def slot_places(routes, expert_count, slot_cap):
    tok_count = routes.shape[0]
    route_width = routes.shape[1]
    flat_routes = routes.reshape(-1)
    onehot = (flat_routes[:, None] == jnp.arange(expert_count, dtype=jnp.int32)[None, :]).astype(
        jnp.int32
    )
    before = jnp.cumsum(onehot, axis=0) - onehot
    position = jnp.sum(before * onehot, axis=1)
    slot_match = (position[:, None] == jnp.arange(slot_cap, dtype=jnp.int32)[None, :]).astype(
        jnp.float32
    )
    placed = onehot.astype(jnp.float32)[:, :, None] * slot_match[:, None, :]
    return placed.reshape(tok_count, route_width, expert_count, slot_cap)


def spread_rows(places, values):
    tok_count = values.shape[0]
    quarter_width = values.shape[1] // 4
    return jnp.einsum(
        "tkec,thf->ehcf",
        places.astype(jnp.bfloat16),
        values.reshape(tok_count, 4, quarter_width),
        preferred_element_type=jnp.float32,
    )


def device_rows(placed):
    return placed.astype(jnp.bfloat16).reshape(
        4 * placed.shape[0], placed.shape[2], placed.shape[3]
    )


def collect(places, returned):
    expert_count = places.shape[2]
    shaped = returned.reshape(expert_count, 4, returned.shape[1], returned.shape[2])
    return jnp.einsum(
        "tkec,ehcf->tkhf", places.astype(jnp.bfloat16), shaped, preferred_element_type=jnp.float32
    )


def contract_cols(left, right):
    return lax.dot_general(
        left, right, (((1,), (1,)), ((), ())), preferred_element_type=jnp.float32
    )


def forward_expert(row_block, w_gate, w_up, w_down):
    proj_width = w_gate.shape[1]
    partials = jnp.concatenate(
        [
            jnp.dot(row_block, w_gate, preferred_element_type=jnp.float32),
            jnp.dot(row_block, w_up, preferred_element_type=jnp.float32),
        ],
        axis=1,
    ).astype(jnp.bfloat16)
    partner_part = partner(partials, "ep", 0)
    pair_sum = partials.astype(jnp.float32) + partner_part.astype(jnp.float32)
    other_pair = partner(pair_sum, "ep", 1)
    summed = pair_sum + other_pair
    hidden = (jax.nn.silu(summed[:, :proj_width]) * summed[:, proj_width:]).astype(jnp.bfloat16)
    return jnp.dot(hidden, w_down, preferred_element_type=jnp.float32).astype(jnp.bfloat16)


def backward_expert(row_block, grad_block, w_gate, w_up, w_down):
    proj_width = w_gate.shape[1]
    partials = jnp.concatenate(
        [
            jnp.dot(row_block, w_gate, preferred_element_type=jnp.float32),
            jnp.dot(row_block, w_up, preferred_element_type=jnp.float32),
        ],
        axis=1,
    ).astype(jnp.bfloat16)
    grad_part = contract_cols(grad_block, w_down).astype(jnp.bfloat16)
    partner_part, partner_grad = partner((partials, grad_part), "ep", 0)
    pair_sum = partials.astype(jnp.float32) + partner_part.astype(jnp.float32)
    pair_grad = grad_part.astype(jnp.float32) + partner_grad.astype(jnp.float32)
    other_sum, other_grad = partner((pair_sum, pair_grad), "ep", 1)
    summed = pair_sum + other_sum
    grad_hidden = pair_grad + other_grad
    gate_value = summed[:, :proj_width]
    up_value = summed[:, proj_width:]
    sigmoid_value = jax.nn.sigmoid(gate_value)
    grad_gate = (
        grad_hidden * up_value * sigmoid_value * (1.0 + gate_value * (1.0 - sigmoid_value))
    ).astype(jnp.bfloat16)
    grad_up = (grad_hidden * gate_value * sigmoid_value).astype(jnp.bfloat16)
    result = contract_cols(grad_gate, w_gate) + contract_cols(grad_up, w_up)
    return result.astype(jnp.bfloat16)


def on_device(
    fwd_tokens,
    fwd_routes,
    fwd_gates,
    bwd_tokens,
    bwd_grads,
    bwd_routes,
    bwd_gates,
    gate_proj,
    up_proj,
    down_proj,
):
    expert_count = lax.axis_size("ep") // 4
    tokens_fwd = fwd_tokens[0]
    tok_count = tokens_fwd.shape[0]
    route_width = fwd_routes.shape[2]
    slot_cap = 3 * tok_count * route_width // (2 * expert_count)
    places_fwd = slot_places(fwd_routes[0], expert_count, slot_cap)
    places_bwd = slot_places(bwd_routes[0], expert_count, slot_cap)
    send_fwd = device_rows(spread_rows(places_fwd, tokens_fwd))
    send_rows = device_rows(spread_rows(places_bwd, bwd_tokens[0]))
    slot_gate = jnp.einsum("tkec,tk->ec", places_bwd, bwd_gates[0], precision=lax.Precision.HIGHEST)
    send_grads = device_rows(spread_rows(places_bwd, bwd_grads[0]) * slot_gate[:, None, :, None])
    recv_fwd = lax.all_to_all(send_fwd, "ep", split_axis=0, concat_axis=0, tiled=True)
    recv_rows, recv_grads = (
        lax.all_to_all(send_rows, "ep", split_axis=0, concat_axis=0, tiled=True),
        lax.all_to_all(send_grads, "ep", split_axis=0, concat_axis=0, tiled=True),
    )
    quarter_width = send_fwd.shape[2]
    w_gate = gate_proj[0, 0]
    w_up = up_proj[0, 0]
    w_down = down_proj[0, 0]
    out_fwd = forward_expert(recv_fwd.reshape(-1, quarter_width), w_gate, w_up, w_down).reshape(
        recv_fwd.shape
    )
    out_bwd = backward_expert(
        recv_rows.reshape(-1, quarter_width),
        recv_grads.reshape(-1, quarter_width),
        w_gate,
        w_up,
        w_down,
    ).reshape(recv_rows.shape)
    back_fwd = lax.all_to_all(out_fwd, "ep", split_axis=0, concat_axis=0, tiled=True)
    back_bwd = lax.all_to_all(out_bwd, "ep", split_axis=0, concat_axis=0, tiled=True)
    gathered = collect(places_fwd, back_fwd)
    mixture = (
        jnp.sum(gathered * fwd_gates[0][:, :, None, None], axis=1)
        .reshape(tok_count, -1)
        .astype(jnp.bfloat16)
    )
    grad_input = (
        jnp.sum(collect(places_bwd, back_bwd), axis=1).reshape(tok_count, -1).astype(jnp.bfloat16)
    )
    handed_forward = shifted(mixture[None], "pp", 1)
    handed_backward = shifted(grad_input[None], "pp", -1)
    return (handed_forward, handed_backward)


def solution(mesh):
    return jax.shard_map(
        on_device,
        mesh=mesh,
        in_specs=(
            P("pp", "ep", None),
            P("pp", "ep", None),
            P("pp", "ep", None),
            P("pp", "ep", None),
            P("pp", "ep", None),
            P("pp", "ep", None),
            P("pp", "ep", None),
            P("pp", "ep", None, None),
            P("pp", "ep", None, None),
            P("pp", "ep", None, None),
        ),
        out_specs=(P("pp", "ep", None), P("pp", "ep", None)),
        check_vma=False,
    )
```

profile of v0, /device:TPU:31, one launch (start us, length us, event | category | flops | bytes accessed | tf_op | source)
XLA Modules:
  0.0 765.7 jit_solution(5984593933473308291)
XLA Ops:
  0.6 0.9 fusion.55
  2.6 1.9 reshape_squeeze.11
  4.5 2.1 convolution_convert_fusion
  6.6 12.0 %all-to-all-start.3 = ((bf16[32,24,1024]{2,1,0:T(8,128)(2,1)}), bf16[32,24,1024]{2,1,0:T(8,128)(2,1)}, u32[]{:S(2)}, u32[]{:S(2)}) async-start(bf16[32,24,1024]{2,1,0:T(8,128)(2,1)} %bitcast.30), calls=%async_computation.3 | async-start | bytes 3145728 | tf_op jit(solution)/shard_map/all_to_all | solution.py:139
  18.8 1.9 reshape_squeeze.9
  20.9 2.1 convolution_convert_fusion.2
  23.0 31.6 %all-to-all-done.3 = bf16[32,24,1024]{2,1,0:T(8,128)(2,1)} async-done(((bf16[32,24,1024]{2,1,0:T(8,128)(2,1)}), bf16[32,24,1024]{2,1,0:T(8,128)(2,1)}, u32[]{:S(2)}, u32[]{:S(2)}) %all-to-all-start.3) | async-done | bytes 1572896 | tf_op jit(solution)/shard_map/all_to_all | solution.py:139
  54.7 9.9 %all-to-all-start = ((bf16[32,24,1024]{2,1,0:T(8,128)(2,1)}), bf16[32,24,1024]{2,1,0:T(8,128)(2,1)}, u32[]{:S(2)}, u32[]{:S(2)}) async-start(bf16[32,24,1024]{2,1,0:T(8,128)(2,1)} %bitcast.5), calls=%async_computation | async-start | bytes 3145728 | tf_op jit(solution)/shard_map/all_to_all | solution.py:137
  64.6 3.3 fusion.25
  67.9 2.8 fusion.31
  70.8 1.7 pad_maximum_fusion.1
  73.0 2.6 reshape_squeeze.10
  76.2 3.4 multiply_convert_fusion
  79.6 23.7 %all-to-all-done = bf16[32,24,1024]{2,1,0:T(8,128)(2,1)} async-done(((bf16[32,24,1024]{2,1,0:T(8,128)(2,1)}), bf16[32,24,1024]{2,1,0:T(8,128)(2,1)}, u32[]{:S(2)}, u32[]{:S(2)}) %all-to-all-start) | async-done | bytes 1572896 | tf_op jit(solution)/shard_map/all_to_all | solution.py:137
  103.3 6.9 all-to-all-start.2
  110.2 4.8 convert_add_fusion
  115.0 2.1 collective-permute-start.6
  117.1 2.9 fusion.22
  119.9 3.3 fusion.28
  123.2 1.7 pad_maximum_fusion
  125.7 23.6 %all-to-all-done.2 = bf16[32,24,1024]{2,1,0:T(8,128)(2,1)} async-done(((bf16[32,24,1024]{2,1,0:T(8,128)(2,1)}), bf16[32,24,1024]{2,1,0:T(8,128)(2,1)}, u32[]{:S(2)}, u32[]{:S(2)}) %all-to-all-start.2) | async-done | bytes 1572896 | tf_op jit(solution)/shard_map/all_to_all | solution.py:140
  149.3 3.3 fusion.34
  153.2 2.5 collective-permute-done.3
  156.0 1.2 collective-permute-start.4
  157.2 4.4 convert_add_fusion.1
  161.6 1.2 collective-permute-start.1
  162.8 338.0 %collective-permute-done.6 = f32[768,1536]{0,1:T(8,128)} collective-permute-done((f32[768,1536]{0,1:T(8,128)}, f32[768,1536]{0,1:T(8,128)}, u32[]{:S(2)}, u32[]{:S(2)}) %collective-permute-start.6) | collective-permute-done | bytes 4718624 | tf_op jit(solution)/shard_map/ppermute | solution.py:14
  500.9 3.7 fusion.80
  504.6 46.7 %collective-permute-done.4 = f32[768,768]{0,1:T(8,128)S(1)} collective-permute-done((f32[768,768]{0,1:T(8,128)S(1)}, f32[768,768]{0,1:T(8,128)S(1)}, u32[]{:S(2)}, u32[]{:S(2)}) %collective-permute-start.4) | collective-permute-done | bytes 2359328 | tf_op jit(solution)/shard_map/ppermute | solution.py:14
  551.3 1.9 fusion.10
  553.2 3.6 add_convert_fusion
  556.8 7.2 all-to-all-start.4
  564.0 114.0 %collective-permute-done.1 = f32[768,1536]{0,1:T(8,128)} collective-permute-done((f32[768,1536]{0,1:T(8,128)}, f32[768,1536]{0,1:T(8,128)}, u32[]{:S(2)}, u32[]{:S(2)}) %collective-permute-start.1) | collective-permute-done | bytes 4718624 | tf_op jit(solution)/shard_map/ppermute | solution.py:14
  678.0 3.7 fusion.79
  681.8 2.6 convolution_convert_fusion.1
  684.4 4.1 all-to-all-done.4
  688.5 6.9 all-to-all-start.1
  695.4 3.8 copy.47
  699.2 2.9 dot_general.60
  702.1 1.4 fusion.1
  703.5 2.4 collective-permute-start.7
  705.9 28.0 %all-to-all-done.1 = bf16[32,24,1024]{2,1,0:T(8,128)(2,1)S(1)} async-done(((bf16[32,24,1024]{2,1,0:T(8,128)(2,1)}), bf16[32,24,1024]{2,1,0:T(8,128)(2,1)S(1)}, u32[]{:S(2)}, u32[]{:S(2)}) %all-to-all-start.1) | async-done | bytes 1572896 | tf_op jit(solution)/shard_map/all_to_all | solution.py:156
  734.3 1.3 copy.22
  735.6 3.8 collective-permute-start.2
  739.4 14.3 %collective-permute-done.7 = bf16[1,128,4096]{2,1,0:T(8,128)(2,1)} collective-permute-done((bf16[1,128,4096]{2,1,0:T(8,128)(2,1)}, bf16[1,128,4096]{2,1,0:T(8,128)(2,1)}, u32[]{:S(2)}, u32[]{:S(2)}) %collective-permute-start.7) | collective-permute-done | bytes 1048608 | tf_op jit(solution)/shard_map/ppermute | solution.py:20
  753.7 8.4 %collective-permute-done.2 = bf16[1,128,4096]{1,2,0:T(8,128)(2,1)S(1)} collective-permute-done((bf16[1,128,4096]{1,2,0:T(8,128)(2,1)}, bf16[1,128,4096]{1,2,0:T(8,128)(2,1)S(1)}, u32[]{:S(2)}, u32[]{:S(2)}) %collective-permute-start.2) | collective-permute-done | bytes 1048608 | tf_op jit(solution)/shard_map/ppermute | solution.py:20
  762.1 1.3 copy.28
  763.4 2.3 copy.49
  (49 shorter events, 4.8 us)
Async XLA Ops:
  0.6 67.3 %copy-start = (bf16[1,1,1024,768]{3,2,1,0:T(8,128)(2,1)S(1)}, bf16[1,1,1024,768]{3,2,1,0:T(8,128)(2,1)}, u32[]{:S(2)}) copy-start(bf16[1,1,1024,768]{3,2,1,0:T(8,128)(2,1)} %param.18) | copy-start | bytes 4718596
  4.5 14.1 %copy-start.10 = (s32[1,128,1]{1,2,0:T(1,128)S(1)}, s32[1,128,1]{1,2,0:T(1,128)}, u32[]{:S(2)}) copy-start(s32[1,128,1]{1,2,0:T(1,128)} %param.11) | copy-start | bytes 1540
  6.6 48.1 %all-to-all-start.3 = ((bf16[32,24,1024]{2,1,0:T(8,128)(2,1)}), bf16[32,24,1024]{2,1,0:T(8,128)(2,1)}, u32[]{:S(2)}, u32[]{:S(2)}) async-start(bf16[32,24,1024]{2,1,0:T(8,128)(2,1)} %bitcast.30), calls=%async_computation.3 | async-start | bytes 3145728 | tf_op jit(solution)/shard_map/all_to_all | solution.py:139
  54.7 48.6 %all-to-all-start = ((bf16[32,24,1024]{2,1,0:T(8,128)(2,1)}), bf16[32,24,1024]{2,1,0:T(8,128)(2,1)}, u32[]{:S(2)}, u32[]{:S(2)}) async-start(bf16[32,24,1024]{2,1,0:T(8,128)(2,1)} %bitcast.5), calls=%async_computation | async-start | bytes 3145728 | tf_op jit(solution)/shard_map/all_to_all | solution.py:137
  70.8 1.8 copy-start.2
  70.8 4.8 copy-start.15
  72.6 37.6 %collective-permute-start.5 = (bf16[768,1536]{0,1:T(8,128)(2,1)}, bf16[768,1536]{0,1:T(8,128)(2,1)}, u32[]{:S(2)}, u32[]{:S(2)}) collective-permute-start(bf16[768,1536]{0,1:T(8,128)(2,1)} %pad_maximum_fusion.1), channel_id=1, source_target_pairs={{0,1},{1,0},{2,3},{3,2},{4,5},{5,4},{6,7},{7,6},{8,9},{9,8},{10,11... | collective-permute-start | bytes 7077896 | tf_op jit(solution)/shard_map/ppermute | solution.py:14
  103.3 46.0 %all-to-all-start.2 = ((bf16[32,24,1024]{2,1,0:T(8,128)(2,1)}), bf16[32,24,1024]{2,1,0:T(8,128)(2,1)}, u32[]{:S(2)}, u32[]{:S(2)}) async-start(bf16[32,24,1024]{2,1,0:T(8,128)(2,1)} %bitcast.108), calls=%async_computation.2 | async-start | bytes 3145728 | tf_op jit(solution)/shard_map/all_to_all | solution.py:140
  110.2 6.9 copy-start.12
  115.0 385.9 %collective-permute-start.6 = (f32[768,1536]{0,1:T(8,128)}, f32[768,1536]{0,1:T(8,128)}, u32[]{:S(2)}, u32[]{:S(2)}) collective-permute-start(f32[768,1536]{0,1:T(8,128)} %convert_add_fusion), channel_id=1, source_target_pairs={{0,2},{2,0},{1,3},{3,1},{4,6},{6,4},{5,7},{7,5},{8,10},{10,8},{9,1... | collective-permute-start | bytes 14155784 | tf_op jit(solution)/shard_map/ppermute | solution.py:14
  119.9 3.3 copy-start.4
  123.2 1.8 copy-start.7
  125.0 32.1 %collective-permute-start = (bf16[768,1536]{0,1:T(8,128)(2,1)}, bf16[768,1536]{0,1:T(8,128)(2,1)}, u32[]{:S(2)}, u32[]{:S(2)}) collective-permute-start(bf16[768,1536]{0,1:T(8,128)(2,1)} %pad_maximum_fusion), channel_id=1, source_target_pairs={{0,1},{1,0},{2,3},{3,2},{4,5},{5,4},{6,7},{7,6},{8,9},{9,8},{10,11... | collective-permute-start | bytes 7077896 | tf_op jit(solution)/shard_map/ppermute | solution.py:14
  152.6 4.6 copy-start.5
  152.6 4.6 copy-start.8
  152.6 3.1 collective-permute-start.3
  156.0 344.9 %copy-start.3 = (bf16[768,768]{0,1:T(8,128)(2,1)S(1)}, bf16[768,768]{0,1:T(8,128)(2,1)}, u32[]{:S(2)}) copy-start(bf16[768,768]{0,1:T(8,128)(2,1)} %copy-done.2) | copy-start | bytes 3538948
  156.0 395.3 %collective-permute-start.4 = (f32[768,768]{0,1:T(8,128)S(1)}, f32[768,768]{0,1:T(8,128)S(1)}, u32[]{:S(2)}, u32[]{:S(2)}) collective-permute-start(f32[768,768]{0,1:T(8,128)S(1)} %convert_add_fusion.2), channel_id=1, source_target_pairs={{0,2},{2,0},{1,3},{3,1},{4,6},{6,4},{5,7},{7,5},{8,10},{10,8},{9,1... | collective-permute-start | bytes 7077896 | tf_op jit(solution)/shard_map/ppermute | solution.py:14
  161.6 516.4 %collective-permute-start.1 = (f32[768,1536]{0,1:T(8,128)}, f32[768,1536]{0,1:T(8,128)}, u32[]{:S(2)}, u32[]{:S(2)}) collective-permute-start(f32[768,1536]{0,1:T(8,128)} %convert_add_fusion.1), channel_id=1, source_target_pairs={{0,2},{2,0},{1,3},{3,1},{4,6},{6,4},{5,7},{7,5},{8,10},{10,8},{9,1... | collective-permute-start | bytes 14155784 | tf_op jit(solution)/shard_map/ppermute | solution.py:14
  504.6 48.6 %copy-start.13 = (bf16[1,1,1024,768]{3,2,1,0:T(8,128)(2,1)S(1)}, bf16[1,1,1024,768]{3,2,1,0:T(8,128)(2,1)}, u32[]{:S(2)}) copy-start(bf16[1,1,1024,768]{3,2,1,0:T(8,128)(2,1)} %param.17) | copy-start | bytes 4718596
  556.8 121.2 %copy-start.6 = (bf16[768,768]{0,1:T(8,128)(2,1)S(1)}, bf16[768,768]{0,1:T(8,128)(2,1)}, u32[]{:S(2)}) copy-start(bf16[768,768]{0,1:T(8,128)(2,1)} %copy-done.4) | copy-start | bytes 3538948
  556.8 121.2 %copy-start.9 = (bf16[768,768]{0,1:T(8,128)(2,1)S(1)}, bf16[768,768]{0,1:T(8,128)(2,1)}, u32[]{:S(2)}) copy-start(bf16[768,768]{0,1:T(8,128)(2,1)} %copy-done.7) | copy-start | bytes 3538948
  556.8 131.7 %all-to-all-start.4 = ((bf16[32,24,1024]{2,1,0:T(8,128)(2,1)}), bf16[32,24,1024]{2,1,0:T(8,128)(2,1)}, u32[]{:S(2)}, u32[]{:S(2)}) async-start(bf16[32,24,1024]{2,1,0:T(8,128)(2,1)} %bitcast.111), calls=%async_computation.4 | async-start | bytes 3145728 | tf_op jit(solution)/shard_map/all_to_all | solution.py:157
  564.0 117.8 %copy-start.14 = (bf16[1,1,768,1024]{3,2,1,0:T(8,128)(2,1)S(1)}, bf16[1,1,768,1024]{3,2,1,0:T(8,128)(2,1)}, u32[]{:S(2)}) copy-start(bf16[1,1,768,1024]{3,2,1,0:T(8,128)(2,1)} %param.19) | copy-start | bytes 4718596
  688.5 45.3 %all-to-all-start.1 = ((bf16[32,24,1024]{2,1,0:T(8,128)(2,1)}), bf16[32,24,1024]{2,1,0:T(8,128)(2,1)S(1)}, u32[]{:S(2)}, u32[]{:S(2)}) async-start(bf16[32,24,1024]{2,1,0:T(8,128)(2,1)} %bitcast.10), calls=%async_computation.1 | async-start | bytes 3145728 | tf_op jit(solution)/shard_map/all_to_all | solution.py:156
  699.2 34.6 %copy-start.11 = (f32[1,128,1]{1,2,0:T(1,128)S(1)}, f32[1,128,1]{1,2,0:T(1,128)}, u32[]{:S(2)}) copy-start(f32[1,128,1]{1,2,0:T(1,128)} %param.12) | copy-start | bytes 1540
  703.5 50.2 %collective-permute-start.7 = (bf16[1,128,4096]{2,1,0:T(8,128)(2,1)}, bf16[1,128,4096]{2,1,0:T(8,128)(2,1)}, u32[]{:S(2)}, u32[]{:S(2)}) collective-permute-start(bf16[1,128,4096]{2,1,0:T(8,128)(2,1)} %fusion.1), channel_id=1, source_target_pairs={{32,0},{64,32},{96,64},{128,96},{160,128},{192,160},{224,192},{33,... | collective-permute-start | bytes 3145736 | tf_op jit(solution)/shard_map/ppermute | solution.py:20
  734.3 31.4 %copy-start.1 = (bf16[1,1,1024,768]{3,2,1,0:T(8,128)(2,1)S(1)}, bf16[1,1,1024,768]{3,2,1,0:T(8,128)(2,1)}, u32[]{:S(2)}) copy-start(bf16[1,1,1024,768]{3,2,1,0:T(8,128)(2,1)} %param.18) | copy-start | bytes 4718596
  735.6 26.5 %collective-permute-start.2 = (bf16[1,128,4096]{1,2,0:T(8,128)(2,1)}, bf16[1,128,4096]{1,2,0:T(8,128)(2,1)S(1)}, u32[]{:S(2)}, u32[]{:S(2)}) collective-permute-start(bf16[1,128,4096]{1,2,0:T(8,128)(2,1)} %bitcast.112), channel_id=1, source_target_pairs={{0,32},{32,64},{64,96},{96,128},{128,160},{160,192},{192,224},{1,3... | collective-permute-start | bytes 3145736 | tf_op jit(solution)/shard_map/ppermute | solution.py:20
where the time goes:
time: 771 us; the launch traced here: 766 us
  waiting for transfers between devices  635 us (82%)
  starting transfers between devices  55.2 us (7%)
  matrix products  33.8 us (4%)
  other arithmetic  22.5 us (3%)
  local copies, waits for them, and re-layouts  18.3 us (2%)
    ppermute x6, waiting for transfers between devices, partner(): return lax.ppermute(block, axis, route)  501 us
    all_to_all x1, waiting for transfers between devices, on_device(): lax.all_to_all(send_rows, 'ep', split_axis=0, concat_axis=0, tiled=True)  31.6 us
    all_to_all x1, waiting for transfers between devices, on_device(): lax.all_to_all(out_fwd, 'ep', split_axis=0, concat_axis=0, tiled=True)  28 us
    all_to_all x1, waiting for transfers between devices, on_device(): lax.all_to_all(send_fwd, 'ep', split_axis=0, concat_axis=0, tiled=True)  23.7 us
    all_to_all x1, waiting for transfers between devices, on_device(): lax.all_to_all(send_grads, 'ep', split_axis=0, concat_axis=0, tiled=True)  23.6 us
    ppermute x2, waiting for transfers between devices, shifted(): return lax.ppermute(shard, axis, pairs)  22.7 us
  transfers between devices with their start and end apart: 13, of which 11 were waited for; matrix products, arithmetic and copies ran while one was open for 8% of the time, Pallas kernels for 0%

commit v1 on v0

--- a/solution.py
+++ b/solution.py
@@ -65,6 +65,35 @@
     return lax.dot_general(
         left, right, (((1,), (1,)), ((), ())), preferred_element_type=jnp.float32
     )
+
+
+def quarter_bits():
+    quarter = lax.axis_index("ep") % 4
+    return quarter // 2, quarter % 2
+
+
+def pick(flag, when_set, when_clear):
+    return jnp.where(flag == 1, when_set, when_clear)
+
+
+def scatter_sum(partials):
+    high, low = quarter_bits()
+    grouped = partials.reshape(2, 2, partials.shape[0] // 4, partials.shape[1])
+    keep_half = pick(high, grouped[1], grouped[0])
+    give_half = pick(high, grouped[0], grouped[1])
+    pair_sum = keep_half.astype(jnp.float32) + partner(give_half, "ep", 1).astype(jnp.float32)
+    keep_group = pick(low, pair_sum[1], pair_sum[0])
+    give_group = pick(low, pair_sum[0], pair_sum[1])
+    return keep_group + partner(give_group, "ep", 0)
+
+
+def gather_groups(block):
+    high, low = quarter_bits()
+    pair = jnp.stack([block, partner(block, "ep", 1)])
+    held = jnp.stack([pair, partner(pair, "ep", 0)], axis=1)
+    held = pick(high, held[::-1], held)
+    held = pick(low, held[:, ::-1], held)
+    return held.reshape(-1, block.shape[1])
 
 
 def forward_expert(row_block, w_gate, w_up, w_down):
@@ -76,11 +105,9 @@
         ],
         axis=1,
     ).astype(jnp.bfloat16)
-    partner_part = partner(partials, "ep", 0)
-    pair_sum = partials.astype(jnp.float32) + partner_part.astype(jnp.float32)
-    other_pair = partner(pair_sum, "ep", 1)
-    summed = pair_sum + other_pair
+    summed = scatter_sum(partials)
     hidden = (jax.nn.silu(summed[:, :proj_width]) * summed[:, proj_width:]).astype(jnp.bfloat16)
+    hidden = gather_groups(hidden)
     return jnp.dot(hidden, w_down, preferred_element_type=jnp.float32).astype(jnp.bfloat16)
 
 
@@ -94,20 +121,19 @@
         axis=1,
     ).astype(jnp.bfloat16)
     grad_part = contract_cols(grad_block, w_down).astype(jnp.bfloat16)
-    partner_part, partner_grad = partner((partials, grad_part), "ep", 0)
-    pair_sum = partials.astype(jnp.float32) + partner_part.astype(jnp.float32)
-    pair_grad = grad_part.astype(jnp.float32) + partner_grad.astype(jnp.float32)
-    other_sum, other_grad = partner((pair_sum, pair_grad), "ep", 1)
-    summed = pair_sum + other_sum
-    grad_hidden = pair_grad + other_grad
+    summed = scatter_sum(jnp.concatenate([partials, grad_part], axis=1))
     gate_value = summed[:, :proj_width]
-    up_value = summed[:, proj_width:]
+    up_value = summed[:, proj_width : 2 * proj_width]
+    grad_hidden = summed[:, 2 * proj_width :]
     sigmoid_value = jax.nn.sigmoid(gate_value)
     grad_gate = (
         grad_hidden * up_value * sigmoid_value * (1.0 + gate_value * (1.0 - sigmoid_value))
     ).astype(jnp.bfloat16)
     grad_up = (grad_hidden * gate_value * sigmoid_value).astype(jnp.bfloat16)
-    result = contract_cols(grad_gate, w_gate) + contract_cols(grad_up, w_up)
+    grads = gather_groups(jnp.concatenate([grad_gate, grad_up], axis=1))
+    result = contract_cols(grads[:, :proj_width], w_gate) + contract_cols(
+        grads[:, proj_width:], w_up
+    )
     return result.astype(jnp.bfloat16)
 
 

time: 771 us -> 459 us (0.60)
  waiting for transfers between devices: 635 us -> 320 us
  local copies, waits for them, and re-layouts: 18.3 us -> 31.4 us
    ppermute x6 -> x8, waiting for transfers between devices: 501 us -> 146 us  [partner(): return lax.ppermute(block, axis, route)]
    all_to_all x1, waiting for transfers between devices: 4.13 us -> 32 us  [on_device(): lax.all_to_all(out_bwd, 'ep', split_axis=0, concat_axis=0, tiled=True)]
    add x5 -> x4, other arithmetic: 16.8 us -> 3.17 us  [the longest x2 2.59 us: scatter_sum(): keep_half.astype(jnp.float32)]
    all_to_all x1, waiting for transfers between devices: 23.7 us -> 34 us  [on_device(): lax.all_to_all(send_fwd, 'ep', split_axis=0, concat_axis=0, tiled=True)]
    convert_element_type x0 -> x2, local copies, waits for them, and re-layouts: none -> 8.25 us  [scatter_sum(): keep_half.astype(jnp.float32)]
  transfers between devices with their start and end apart: 13 -> 15, of which waited for: 11 -> 12; matrix products, arithmetic and copies ran while one was open for 8% -> 15% of each run, Pallas kernels for 0% -> 0%
where the time goes in v1:
time: 459 us; the launch traced here: 455 us
  waiting for transfers between devices  320 us (70%)
  starting transfers between devices  54.4 us (12%)
  matrix products  32.5 us (7%)
  local copies, waits for them, and re-layouts  31.4 us (7%)
  other arithmetic  15.9 us (3%)
    ppermute x8, waiting for transfers between devices, partner(): return lax.ppermute(block, axis, route)  146 us
    all_to_all x1, waiting for transfers between devices, on_device(): lax.all_to_all(send_fwd, 'ep', split_axis=0, concat_axis=0, tiled=True)  34 us
    all_to_all x1, waiting for transfers between devices, on_device(): lax.all_to_all(send_rows, 'ep', split_axis=0, concat_axis=0, tiled=True)  32.4 us
    all_to_all x1, waiting for transfers between devices, on_device(): lax.all_to_all(out_bwd, 'ep', split_axis=0, concat_axis=0, tiled=True)  32 us
    all_to_all x1, waiting for transfers between devices, on_device(): lax.all_to_all(out_fwd, 'ep', split_axis=0, concat_axis=0, tiled=True)  30.9 us
    ppermute x2, waiting for transfers between devices, shifted(): return lax.ppermute(shard, axis, pairs)  23.5 us
    all_to_all x1, waiting for transfers between devices, on_device(): lax.all_to_all(send_grads, 'ep', split_axis=0, concat_axis=0, tiled=True)  21 us
    all_to_all x1, starting transfers between devices, on_device(): lax.all_to_all(send_rows, 'ep', split_axis=0, concat_axis=0, tiled=True)  12.1 us
  transfers between devices with their start and end apart: 15, of which 12 were waited for; matrix products, arithmetic and copies ran while one was open for 15% of the time, Pallas kernels for 0%

profile of v1, /device:TPU:31, one launch (start us, length us, event | category | flops | bytes accessed | tf_op | source)
XLA Modules:
  0.0 455.2 jit_solution(9422874228060646365)
XLA Ops:
  2.6 1.9 reshape_squeeze.10
  4.5 2.1 convolution_convert_fusion
  6.5 12.1 %all-to-all-start.2 = ((bf16[32,24,1024]{2,1,0:T(8,128)(2,1)}), bf16[32,24,1024]{2,1,0:T(8,128)(2,1)}, u32[]{:S(2)}, u32[]{:S(2)}) async-start(bf16[32,24,1024]{2,1,0:T(8,128)(2,1)} %bitcast.30), calls=%async_computation.2 | async-start | bytes 3145728 | tf_op jit(solution)/shard_map/all_to_all | solution.py:165
  19.0 1.9 reshape_squeeze.9
  21.0 2.1 convolution_convert_fusion.2
  23.1 32.4 %all-to-all-done.2 = bf16[32,24,1024]{2,1,0:T(8,128)(2,1)} async-done(((bf16[32,24,1024]{2,1,0:T(8,128)(2,1)}), bf16[32,24,1024]{2,1,0:T(8,128)(2,1)}, u32[]{:S(2)}, u32[]{:S(2)}) %all-to-all-start.2) | async-done | bytes 1572896 | tf_op jit(solution)/shard_map/all_to_all | solution.py:165
  55.5 9.3 %all-to-all-start = ((bf16[32,24,1024]{2,1,0:T(8,128)(2,1)}), bf16[32,24,1024]{2,1,0:T(8,128)(2,1)}, u32[]{:S(2)}, u32[]{:S(2)}) async-start(bf16[32,24,1024]{2,1,0:T(8,128)(2,1)} %bitcast.5), calls=%async_computation | async-start | bytes 3145728 | tf_op jit(solution)/shard_map/all_to_all | solution.py:163
  64.8 1.9 reshape_squeeze.11
  67.3 2.1 multiply_convert_fusion
  69.4 34.0 %all-to-all-done = bf16[32,24,1024]{2,1,0:T(8,128)(2,1)} async-done(((bf16[32,24,1024]{2,1,0:T(8,128)(2,1)}), bf16[32,24,1024]{2,1,0:T(8,128)(2,1)}, u32[]{:S(2)}, u32[]{:S(2)}) %all-to-all-start) | async-done | bytes 1572896 | tf_op jit(solution)/shard_map/all_to_all | solution.py:163
  103.4 7.1 %all-to-all-start.3 = ((bf16[32,24,1024]{2,1,0:T(8,128)(2,1)}), bf16[32,24,1024]{2,1,0:T(8,128)(2,1)}, u32[]{:S(2)}, u32[]{:S(2)}) async-start(bf16[32,24,1024]{2,1,0:T(8,128)(2,1)} %bitcast.39), calls=%async_computation.3 | async-start | bytes 3145728 | tf_op jit(solution)/shard_map/all_to_all | solution.py:166
  110.6 3.0 fusion.17
  113.5 2.9 fusion.23
  116.4 1.9 broadcast_select_fusion.1
  118.3 1.5 copy.27
  119.8 2.1 collective-permute-start
  121.9 3.0 fusion.20
  124.8 3.9 fusion.26
  128.8 21.0 %all-to-all-done.3 = bf16[32,24,1024]{2,1,0:T(8,128)(2,1)} async-done(((bf16[32,24,1024]{2,1,0:T(8,128)(2,1)}), bf16[32,24,1024]{2,1,0:T(8,128)(2,1)}, u32[]{:S(2)}, u32[]{:S(2)}) %all-to-all-start.3) | async-done | bytes 1572896 | tf_op jit(solution)/shard_map/all_to_all | solution.py:166
  149.8 3.4 fusion.29
  153.6 2.2 broadcast_select_fusion
  155.8 2.4 copy.35
  158.8 5.2 %copy.34 = f32[384,2304]{1,0:T(8,128)} copy(f32[384,2304]{0,1:T(8,128)} %get-tuple-element.5) | data formatting | bytes 7077888 | tf_op jit(solution)/shard_map/convert_element_type | solution.py:84
  163.9 3.1 copy.26
  167.0 68.8 %collective-permute-done = bf16[2,192,1536]{2,1,0:T(8,128)(2,1)} collective-permute-done((bf16[2,192,1536]{2,1,0:T(8,128)(2,1)}, bf16[2,192,1536]{2,1,0:T(8,128)(2,1)}, u32[]{:S(2)}, u32[]{:S(2)}) %collective-permute-start) | collective-permute-done | bytes 1179680 | tf_op jit(solution)/shard_map/ppermute | solution.py:14
  235.8 2.3 convert_add_fusion.1
  238.9 34.8 %collective-permute-done.5 = bf16[2,192,2304]{2,1,0:T(8,128)(2,1)S(1)} collective-permute-done((bf16[2,192,2304]{2,1,0:T(8,128)(2,1)}, bf16[2,192,2304]{2,1,0:T(8,128)(2,1)S(1)}, u32[]{:S(2)}, u32[]{:S(2)}) %collective-permute-start.5) | collective-permute-done | bytes 1769504 | tf_op jit(solution)/shard_map/ppermute | solution.py:14
  275.4 14.0 %collective-permute-done.2 = bf16[192,768]{1,0:T(8,128)(2,1)S(1)} collective-permute-done((bf16[192,768]{1,0:T(8,128)(2,1)S(1)}, bf16[192,768]{1,0:T(8,128)(2,1)S(1)}, u32[]{:S(2)}, u32[]{:S(2)}) %collective-permute-start.2) | collective-permute-done | bytes 294944 | tf_op jit(solution)/shard_map/ppermute | solution.py:14
  292.0 27.7 %collective-permute-done.7 = bf16[192,1536]{1,0:T(8,128)(2,1)S(1)} collective-permute-done((bf16[192,1536]{1,0:T(8,128)(2,1)S(1)}, bf16[192,1536]{1,0:T(8,128)(2,1)S(1)}, u32[]{:S(2)}, u32[]{:S(2)}) %collective-permute-start.7) | collective-permute-done | bytes 589856 | tf_op jit(solution)/shard_map/ppermute | solution.py:14
  319.6 1.6 fusion.74
  323.3 2.6 convolution_convert_fusion.1
  325.8 8.4 %all-to-all-start.1 = ((bf16[32,24,1024]{2,1,0:T(8,128)(2,1)}), bf16[32,24,1024]{2,1,0:T(8,128)(2,1)S(1)}, u32[]{:S(2)}, u32[]{:S(2)}) async-start(bf16[32,24,1024]{2,1,0:T(8,128)(2,1)} %bitcast.140), calls=%async_computation.1 | async-start | bytes 3145728 | tf_op jit(solution)/shard_map/all_to_all | solution.py:182
  334.3 1.8 pad_maximum_fusion.1
  337.2 1.4 fusion.11
  338.7 2.6 add_convert_fusion
  341.2 30.9 %all-to-all-done.1 = bf16[32,24,1024]{2,1,0:T(8,128)(2,1)S(1)} async-done(((bf16[32,24,1024]{2,1,0:T(8,128)(2,1)}), bf16[32,24,1024]{2,1,0:T(8,128)(2,1)S(1)}, u32[]{:S(2)}, u32[]{:S(2)}) %all-to-all-start.1) | async-done | bytes 1572896 | tf_op jit(solution)/shard_map/all_to_all | solution.py:182
  372.2 8.3 %all-to-all-start.4 = ((bf16[32,24,1024]{2,1,0:T(8,128)(2,1)}), bf16[32,24,1024]{2,1,0:T(8,128)(2,1)}, u32[]{:S(2)}, u32[]{:S(2)}) async-start(bf16[32,24,1024]{2,1,0:T(8,128)(2,1)} %bitcast.141), calls=%async_computation.4 | async-start | bytes 3145728 | tf_op jit(solution)/shard_map/all_to_all | solution.py:183
  380.5 1.5 fusion.2
  382.0 2.3 copy.30
  384.2 1.9 collective-permute-start.4
  386.1 32.0 %all-to-all-done.4 = bf16[32,24,1024]{2,1,0:T(8,128)(2,1)} async-done(((bf16[32,24,1024]{2,1,0:T(8,128)(2,1)}), bf16[32,24,1024]{2,1,0:T(8,128)(2,1)}, u32[]{:S(2)}, u32[]{:S(2)}) %all-to-all-start.4) | async-done | bytes 1572896 | tf_op jit(solution)/shard_map/all_to_all | solution.py:183
  418.1 3.8 copy.56
  421.9 2.8 dot_general.60
  424.8 1.5 fusion.1
  426.2 2.3 collective-permute-start.9
  428.5 8.8 %collective-permute-done.4 = bf16[1,128,4096]{1,2,0:T(8,128)(2,1)} collective-permute-done((bf16[1,128,4096]{1,2,0:T(8,128)(2,1)}, bf16[1,128,4096]{1,2,0:T(8,128)(2,1)}, u32[]{:S(2)}, u32[]{:S(2)}) %collective-permute-start.4) | collective-permute-done | bytes 1048608 | tf_op jit(solution)/shard_map/ppermute | solution.py:20
  437.3 2.3 copy.38
  439.6 14.7 %collective-permute-done.9 = bf16[1,128,4096]{2,1,0:T(8,128)(2,1)S(1)} collective-permute-done((bf16[1,128,4096]{2,1,0:T(8,128)(2,1)}, bf16[1,128,4096]{2,1,0:T(8,128)(2,1)S(1)}, u32[]{:S(2)}, u32[]{:S(2)}) %collective-permute-start.9) | collective-permute-done | bytes 1048608 | tf_op jit(solution)/shard_map/ppermute | solution.py:20
  (61 shorter events, 13.2 us)
Async XLA Ops:
  0.6 109.9 %copy-start = (bf16[1,1,1024,768]{3,2,1,0:T(8,128)(2,1)S(1)}, bf16[1,1,1024,768]{3,2,1,0:T(8,128)(2,1)}, u32[]{:S(2)}) copy-start(bf16[1,1,1024,768]{3,2,1,0:T(8,128)(2,1)} %param.17) | copy-start | bytes 4718596
  6.5 12.1 %copy-start.3 = (s32[1,128,1]{1,2,0:T(1,128)S(1)}, s32[1,128,1]{1,2,0:T(1,128)}, u32[]{:S(2)}) copy-start(s32[1,128,1]{1,2,0:T(1,128)} %param.11) | copy-start | bytes 1540
  6.5 49.0 %all-to-all-start.2 = ((bf16[32,24,1024]{2,1,0:T(8,128)(2,1)}), bf16[32,24,1024]{2,1,0:T(8,128)(2,1)}, u32[]{:S(2)}, u32[]{:S(2)}) async-start(bf16[32,24,1024]{2,1,0:T(8,128)(2,1)} %bitcast.30), calls=%async_computation.2 | async-start | bytes 3145728 | tf_op jit(solution)/shard_map/all_to_all | solution.py:165
  55.5 47.9 %all-to-all-start = ((bf16[32,24,1024]{2,1,0:T(8,128)(2,1)}), bf16[32,24,1024]{2,1,0:T(8,128)(2,1)}, u32[]{:S(2)}, u32[]{:S(2)}) async-start(bf16[32,24,1024]{2,1,0:T(8,128)(2,1)} %bitcast.5), calls=%async_computation | async-start | bytes 3145728 | tf_op jit(solution)/shard_map/all_to_all | solution.py:163
  64.8 1.9 copy-start.9
  103.4 46.4 %all-to-all-start.3 = ((bf16[32,24,1024]{2,1,0:T(8,128)(2,1)}), bf16[32,24,1024]{2,1,0:T(8,128)(2,1)}, u32[]{:S(2)}, u32[]{:S(2)}) async-start(bf16[32,24,1024]{2,1,0:T(8,128)(2,1)} %bitcast.39), calls=%async_computation.3 | async-start | bytes 3145728 | tf_op jit(solution)/shard_map/all_to_all | solution.py:166
  110.6 3.0 copy-start.6
  119.8 116.1 %collective-permute-start = (bf16[2,192,1536]{2,1,0:T(8,128)(2,1)}, bf16[2,192,1536]{2,1,0:T(8,128)(2,1)}, u32[]{:S(2)}, u32[]{:S(2)}) collective-permute-start(bf16[2,192,1536]{2,1,0:T(8,128)(2,1)} %bitcast.142), channel_id=1, source_target_pairs={{0,2},{2,0},{1,3},{3,1},{4,6},{6,4},{5,7},{7,5},{8,10},{10,8},{9,1... | collective-permute-start | bytes 3538952 | tf_op jit(solution)/shard_map/ppermute | solution.py:14
  121.9 3.0 copy-start.7
  149.8 3.4 copy-start.2
  158.1 115.5 %collective-permute-start.5 = (bf16[2,192,2304]{2,1,0:T(8,128)(2,1)}, bf16[2,192,2304]{2,1,0:T(8,128)(2,1)S(1)}, u32[]{:S(2)}, u32[]{:S(2)}) collective-permute-start(bf16[2,192,2304]{2,1,0:T(8,128)(2,1)} %bitcast.139), channel_id=1, source_target_pairs={{0,2},{2,0},{1,3},{3,1},{4,6},{6,4},{5,7},{7,5},{8,10},{10,8},{9,1... | collective-permute-start | bytes 5308424 | tf_op jit(solution)/shard_map/ppermute | solution.py:14
  238.2 35.5 %copy-start.1 = (f32[384,2304]{1,0:T(8,128)S(1)}, f32[384,2304]{1,0:T(8,128)}, u32[]{:S(2)}) copy-start(f32[384,2304]{1,0:T(8,128)} %copy.34) | copy-start | bytes 10616836
  238.3 36.4 %collective-permute-start.1 = (f32[192,1536]{1,0:T(8,128)S(1)}, f32[192,1536]{1,0:T(8,128)S(1)}, u32[]{:S(2)}, u32[]{:S(2)}) collective-permute-start(f32[192,1536]{1,0:T(8,128)S(1)} %select_bitcast_fusion.1), channel_id=1, source_target_pairs={{0,1},{1,0},{2,3},{3,2},{4,5},{5,4},{6,7},{7,6},{8,9},{9,8},{10,11... | collective-permute-start | bytes 3538952 | tf_op jit(solution)/shard_map/ppermute | solution.py:14
  274.1 15.9 %collective-permute-start.6 = (f32[192,2304]{1,0:T(8,128)S(1)}, f32[192,2304]{1,0:T(8,128)S(1)}, u32[]{:S(2)}, u32[]{:S(2)}) collective-permute-start(f32[192,2304]{1,0:T(8,128)S(1)} %select_bitcast_fusion), channel_id=1, source_target_pairs={{0,1},{1,0},{2,3},{3,2},{4,5},{5,4},{6,7},{7,6},{8,9},{9,8},{10,11... | collective-permute-start | bytes 5308424 | tf_op jit(solution)/shard_map/ppermute | solution.py:14
  275.1 14.3 %collective-permute-start.2 = (bf16[192,768]{1,0:T(8,128)(2,1)S(1)}, bf16[192,768]{1,0:T(8,128)(2,1)S(1)}, u32[]{:S(2)}, u32[]{:S(2)}) collective-permute-start(bf16[192,768]{1,0:T(8,128)(2,1)S(1)} %fusion.44), channel_id=1, source_target_pairs={{0,2},{2,0},{1,3},{3,1},{4,6},{6,4},{5,7},{7,5},{8,10},{10,8},{9,1... | collective-permute-start | bytes 884744 | tf_op jit(solution)/shard_map/ppermute | solution.py:14
  289.5 2.2 collective-permute-start.3
  290.7 28.9 %collective-permute-start.7 = (bf16[192,1536]{1,0:T(8,128)(2,1)S(1)}, bf16[192,1536]{1,0:T(8,128)(2,1)S(1)}, u32[]{:S(2)}, u32[]{:S(2)}) collective-permute-start(bf16[192,1536]{1,0:T(8,128)(2,1)S(1)} %get-tuple-element.13), channel_id=1, source_target_pairs={{0,2},{2,0},{1,3},{3,1},{4,6},{6,4},{5,7},{7,5},{8,10},{10,8},{9,1... | collective-permute-start | bytes 1769480 | tf_op jit(solution)/shard_map/ppermute | solution.py:14
  321.2 13.1 %collective-permute-start.8 = (bf16[2,192,1536]{2,1,0:T(8,128)(2,1)}, bf16[2,192,1536]{2,1,0:T(8,128)(2,1)}, u32[]{:S(2)}, u32[]{:S(2)}) collective-permute-start(bf16[2,192,1536]{2,1,0:T(8,128)(2,1)} %get-tuple-element.11), channel_id=1, source_target_pairs={{0,1},{1,0},{2,3},{3,2},{4,5},{5,4},{6,7},{7,6},{8,9},{9,8},{10,11... | collective-permute-start | bytes 3538952 | tf_op jit(solution)/shard_map/ppermute | solution.py:14
  321.9 1.4 copy-start.5
  325.8 46.3 %all-to-all-start.1 = ((bf16[32,24,1024]{2,1,0:T(8,128)(2,1)}), bf16[32,24,1024]{2,1,0:T(8,128)(2,1)S(1)}, u32[]{:S(2)}, u32[]{:S(2)}) async-start(bf16[32,24,1024]{2,1,0:T(8,128)(2,1)} %bitcast.140), calls=%async_computation.1 | async-start | bytes 3145728 | tf_op jit(solution)/shard_map/all_to_all | solution.py:182
  337.2 1.4 copy-start.8
  372.2 8.3 %copy-start.4 = (f32[1,128,1]{1,2,0:T(1,128)S(1)}, f32[1,128,1]{1,2,0:T(1,128)}, u32[]{:S(2)}) copy-start(f32[1,128,1]{1,2,0:T(1,128)} %param.12) | copy-start | bytes 1540
  372.2 46.0 %all-to-all-start.4 = ((bf16[32,24,1024]{2,1,0:T(8,128)(2,1)}), bf16[32,24,1024]{2,1,0:T(8,128)(2,1)}, u32[]{:S(2)}, u32[]{:S(2)}) async-start(bf16[32,24,1024]{2,1,0:T(8,128)(2,1)} %bitcast.141), calls=%async_computation.4 | async-start | bytes 3145728 | tf_op jit(solution)/shard_map/all_to_all | solution.py:183
  384.2 53.1 %collective-permute-start.4 = (bf16[1,128,4096]{1,2,0:T(8,128)(2,1)}, bf16[1,128,4096]{1,2,0:T(8,128)(2,1)}, u32[]{:S(2)}, u32[]{:S(2)}) collective-permute-start(bf16[1,128,4096]{1,2,0:T(8,128)(2,1)} %bitcast.24), channel_id=1, source_target_pairs={{0,32},{32,64},{64,96},{96,128},{128,160},{160,192},{192,224},{1,3... | collective-permute-start | bytes 3145736 | tf_op jit(solution)/shard_map/ppermute | solution.py:20
  426.2 28.0 %collective-permute-start.9 = (bf16[1,128,4096]{2,1,0:T(8,128)(2,1)}, bf16[1,128,4096]{2,1,0:T(8,128)(2,1)S(1)}, u32[]{:S(2)}, u32[]{:S(2)}) collective-permute-start(bf16[1,128,4096]{2,1,0:T(8,128)(2,1)} %fusion.1), channel_id=1, source_target_pairs={{32,0},{64,32},{96,64},{128,96},{160,128},{192,160},{224,192},{33,... | collective-permute-start | bytes 3145736 | tf_op jit(solution)/shard_map/ppermute | solution.py:20

commit v2 on v1

--- a/solution.py
+++ b/solution.py
@@ -79,12 +79,12 @@
 def scatter_sum(partials):
     high, low = quarter_bits()
     grouped = partials.reshape(2, 2, partials.shape[0] // 4, partials.shape[1])
-    keep_half = pick(high, grouped[1], grouped[0])
-    give_half = pick(high, grouped[0], grouped[1])
-    pair_sum = keep_half.astype(jnp.float32) + partner(give_half, "ep", 1).astype(jnp.float32)
-    keep_group = pick(low, pair_sum[1], pair_sum[0])
-    give_group = pick(low, pair_sum[0], pair_sum[1])
-    return keep_group + partner(give_group, "ep", 0)
+    keep_pair = pick(low, grouped[:, 1], grouped[:, 0])
+    give_pair = pick(low, grouped[:, 0], grouped[:, 1])
+    pair_sum = keep_pair.astype(jnp.float32) + partner(give_pair, "ep", 0).astype(jnp.float32)
+    keep_group = pick(high, pair_sum[1], pair_sum[0])
+    give_group = pick(high, pair_sum[0], pair_sum[1])
+    return keep_group + partner(give_group, "ep", 1)
 
 
 def gather_groups(block):
@@ -160,11 +160,17 @@
     send_rows = device_rows(spread_rows(places_bwd, bwd_tokens[0]))
     slot_gate = jnp.einsum("tkec,tk->ec", places_bwd, bwd_gates[0], precision=lax.Precision.HIGHEST)
     send_grads = device_rows(spread_rows(places_bwd, bwd_grads[0]) * slot_gate[:, None, :, None])
-    recv_fwd = lax.all_to_all(send_fwd, "ep", split_axis=0, concat_axis=0, tiled=True)
-    recv_rows, recv_grads = (
-        lax.all_to_all(send_rows, "ep", split_axis=0, concat_axis=0, tiled=True),
-        lax.all_to_all(send_grads, "ep", split_axis=0, concat_axis=0, tiled=True),
-    )
+    slot_cap_fwd = send_fwd.shape[1]
+    received = lax.all_to_all(
+        jnp.concatenate([send_fwd, send_rows, send_grads], axis=1),
+        "ep",
+        split_axis=0,
+        concat_axis=0,
+        tiled=True,
+    )
+    recv_fwd = received[:, :slot_cap_fwd]
+    recv_rows = received[:, slot_cap_fwd : 2 * slot_cap_fwd]
+    recv_grads = received[:, 2 * slot_cap_fwd :]
     quarter_width = send_fwd.shape[2]
     w_gate = gate_proj[0, 0]
     w_up = up_proj[0, 0]
@@ -179,8 +185,11 @@
         w_up,
         w_down,
     ).reshape(recv_rows.shape)
-    back_fwd = lax.all_to_all(out_fwd, "ep", split_axis=0, concat_axis=0, tiled=True)
-    back_bwd = lax.all_to_all(out_bwd, "ep", split_axis=0, concat_axis=0, tiled=True)
+    back = lax.all_to_all(
+        jnp.concatenate([out_fwd, out_bwd], axis=1), "ep", split_axis=0, concat_axis=0, tiled=True
+    )
+    back_fwd = back[:, :slot_cap_fwd]
+    back_bwd = back[:, slot_cap_fwd:]
     gathered = collect(places_fwd, back_fwd)
     mixture = (
         jnp.sum(gathered * fwd_gates[0][:, :, None, None], axis=1)

time: 459 us -> 464 us (1.011)
  blocking collectives: 0 us -> 70.1 us
  waiting for transfers between devices: 320 us -> 284 us
  starting transfers between devices: 54.4 us -> 34.8 us
  matrix products: 32.5 us -> 19.3 us
    all_to_all x0 -> x1, blocking collectives: none -> 70.1 us  [on_device(): lax.all_to_all(jnp.concatenate([out_fwd, out_bwd], axis=1), 'ep', split_a...]
    all_to_all x5 -> x1, waiting for transfers between devices: 150 us -> 102 us  [on_device(): lax.all_to_all(jnp.concatenate([send_fwd, send_rows, send_grads], axis=1)...]
    all_to_all x5 -> x1, starting transfers between devices: 45.2 us -> 12 us  [on_device(): lax.all_to_all(jnp.concatenate([send_fwd, send_rows, send_grads], axis=1)...]
    ppermute x8, waiting for transfers between devices: 146 us -> 159 us  [partner(): return lax.ppermute(block, axis, route)]
    ppermute x2, starting transfers between devices: 4.16 us -> 13.4 us  [shifted(): return lax.ppermute(shard, axis, pairs)]
    convert_element_type x2 -> x0, local copies, waits for them, and re-layouts: 8.25 us -> none  [scatter_sum(): keep_half.astype(jnp.float32)]
    concatenate x0 -> x1, local copies, waits for them, and re-layouts: none -> 5.85 us  [backward_expert(): summed = scatter_sum(jnp.concatenate([partials, grad_part], axis=1))]
  transfers between devices with their start and end apart: 15 -> 11, of which waited for: 12 -> 7; matrix products, arithmetic and copies ran while one was open for 15% -> 5% of each run, Pallas kernels for 0% -> 0%
where the time goes in v2:
time: 464 us; the launch traced here: 457 us
  waiting for transfers between devices  284 us (61%)
  blocking collectives  70.1 us (15%)
  starting transfers between devices  34.8 us (7%)
  local copies, waits for them, and re-layouts  28.9 us (6%)
  other arithmetic  19.7 us (4%)
  matrix products  19.3 us (4%)
    ppermute x8, waiting for transfers between devices, partner(): return lax.ppermute(block, axis, route)  159 us
    all_to_all x1, waiting for transfers between devices, on_device(): lax.all_to_all(jnp.concatenate([send_fwd, send_rows, send_grads], axis=1)...  102 us
    all_to_all x1, blocking collectives, on_device(): lax.all_to_all(jnp.concatenate([out_fwd, out_bwd], axis=1), 'ep', split_a...  70.1 us
    ppermute x2, waiting for transfers between devices, shifted(): return lax.ppermute(shard, axis, pairs)  22.4 us
    ppermute x2, starting transfers between devices, shifted(): return lax.ppermute(shard, axis, pairs)  13.4 us
    all_to_all x1, starting transfers between devices, on_device(): lax.all_to_all(jnp.concatenate([send_fwd, send_rows, send_grads], axis=1)...  12 us
    ppermute x8, starting transfers between devices, partner(): return lax.ppermute(block, axis, route)  9.37 us
  transfers between devices with their start and end apart: 11, of which 7 were waited for; matrix products, arithmetic and copies ran while one was open for 5% of the time, Pallas kernels for 0%

profile of v2, /device:TPU:31, one launch (start us, length us, event | category | flops | bytes accessed | tf_op | source)
XLA Modules:
  0.0 457.5 jit_solution(15082437595438432944)
XLA Ops:
  0.7 0.9 fusion.53
  1.7 0.8 select_reduce_fusion
  2.6 2.7 reshape_squeeze.11
  5.3 1.6 reshape_squeeze.10
  7.4 2.2 convolution_convert_fusion.1
  10.1 2.7 reshape_squeeze.9
  12.8 2.2 multiply_convert_fusion
  15.1 0.9 convolution_convert_fusion.2
  16.0 2.4 pad_maximum_fusion
  18.5 12.0 %all-to-all-start = ((bf16[32,72,1024]{2,1,0:T(8,128)(2,1)}), bf16[32,72,1024]{2,1,0:T(8,128)(2,1)}, u32[]{:S(2)}, u32[]{:S(2)}) async-start(bf16[32,72,1024]{2,1,0:T(8,128)(2,1)} %pad_maximum_fusion), calls=%async_computation | async-start | bytes 9437184 | tf_op jit(solution)/shard_map/all_to_all | solution.py:164
  30.5 102.4 %all-to-all-done = bf16[32,72,1024]{2,1,0:T(8,128)(2,1)} async-done(((bf16[32,72,1024]{2,1,0:T(8,128)(2,1)}), bf16[32,72,1024]{2,1,0:T(8,128)(2,1)}, u32[]{:S(2)}, u32[]{:S(2)}) %all-to-all-start) | async-done | bytes 4718624 | tf_op jit(solution)/shard_map/all_to_all | solution.py:164
  132.8 2.9 fusion.77
  135.7 1.4 fusion.26
  137.1 1.4 fusion.29
  138.5 1.5 fusion.17
  140.0 1.5 fusion.20
  141.6 1.3 fusion.32
  142.9 1.1 collective-permute-start
  144.0 1.4 fusion.23
  145.4 2.1 pad_maximum_fusion.1
  147.5 5.8 %copy.32 = bf16[768,2304]{1,0:T(8,128)(2,1)} copy(bf16[768,2304]{0,1:T(8,128)(2,1)} %pad_maximum_fusion.1) | data formatting | bytes 7077888 | tf_op jit(solution)/shard_map/concatenate | solution.py:124
  153.4 3.4 select_bitcast_fusion.1
  157.3 2.1 convert_add_fusion.1
  159.5 4.0 collective-permute-start.1
  163.5 2.0 convert_add_fusion
  165.7 1.8 collective-permute-start.5
  167.6 85.4 %collective-permute-done.1 = f32[192,1536]{1,0:T(8,128)S(1)} collective-permute-done((f32[192,1536]{1,0:T(8,128)S(1)}, f32[192,1536]{1,0:T(8,128)S(1)}, u32[]{:S(2)}, u32[]{:S(2)}) %collective-permute-start.1) | collective-permute-done | bytes 1179680 | tf_op jit(solution)/shard_map/ppermute | solution.py:14
  253.6 43.7 %collective-permute-done.5 = f32[192,2304]{1,0:T(8,128)S(1)} collective-permute-done((f32[192,2304]{1,0:T(8,128)S(1)}, f32[192,2304]{1,0:T(8,128)S(1)}, u32[]{:S(2)}, u32[]{:S(2)}) %collective-permute-start.5) | collective-permute-done | bytes 1769504 | tf_op jit(solution)/shard_map/ppermute | solution.py:14
  298.2 18.0 %collective-permute-done.2 = bf16[192,768]{1,0:T(8,128)(2,1)S(1)} collective-permute-done((bf16[192,768]{1,0:T(8,128)(2,1)S(1)}, bf16[192,768]{1,0:T(8,128)(2,1)S(1)}, u32[]{:S(2)}, u32[]{:S(2)}) %collective-permute-start.2) | collective-permute-done | bytes 294944 | tf_op jit(solution)/shard_map/ppermute | solution.py:14
  316.3 0.9 collective-permute-start.3
  317.2 11.7 %collective-permute-done.6 = bf16[192,1536]{1,0:T(8,128)(2,1)S(1)} collective-permute-done((bf16[192,1536]{1,0:T(8,128)(2,1)S(1)}, bf16[192,1536]{1,0:T(8,128)(2,1)S(1)}, u32[]{:S(2)}, u32[]{:S(2)}) %collective-permute-start.6) | collective-permute-done | bytes 589856 | tf_op jit(solution)/shard_map/ppermute | solution.py:14
  329.0 0.9 collective-permute-start.7
  330.6 1.3 copy-done.9
  331.9 1.4 convolution_convert_fusion
  334.7 1.4 fusion.15
  336.1 1.4 add_convert_fusion
  338.0 70.1 %all_to_all.10 = bf16[32,48,1024]{2,1,0:T(8,128)(2,1)S(1)} all-to-all(bf16[32,48,1024]{2,1,0:T(8,128)(2,1)S(1)} %pad_maximum_fusion.2), channel_id=1, replica_groups=mesh['pp'=8,'ep'=32] {'ep'}, dimensions={0} | all-to-all | bytes 6291456 | tf_op jit(solution)/shard_map/all_to_all | solution.py:188
  408.1 1.5 fusion.78
  409.6 2.4 copy.62
  411.9 2.8 dot_general.63
  414.8 1.5 fusion.1
  416.3 2.4 collective-permute-start.9
  419.1 1.3 copy.37
  420.4 11.1 %collective-permute-start.8 = (bf16[1,128,4096]{1,2,0:T(8,128)(2,1)}, bf16[1,128,4096]{1,2,0:T(8,128)(2,1)S(1)}, u32[]{:S(2)}, u32[]{:S(2)}) collective-permute-start(bf16[1,128,4096]{1,2,0:T(8,128)(2,1)} %bitcast.195), channel_id=1, source_target_pairs={{0,32},{32,64},{64,96},{96,128},{128,160},{160,192},{192,224},{1,3... | collective-permute-start | bytes 3145736 | tf_op jit(solution)/shard_map/ppermute | solution.py:20
  431.5 19.7 %collective-permute-done.9 = bf16[1,128,4096]{2,1,0:T(8,128)(2,1)} collective-permute-done((bf16[1,128,4096]{2,1,0:T(8,128)(2,1)}, bf16[1,128,4096]{2,1,0:T(8,128)(2,1)}, u32[]{:S(2)}, u32[]{:S(2)}) %collective-permute-start.9) | collective-permute-done | bytes 1048608 | tf_op jit(solution)/shard_map/ppermute | solution.py:20
  451.2 2.7 collective-permute-done.8
  453.9 1.3 copy.39
  455.2 2.3 copy.64
  (61 shorter events, 6.8 us)
Async XLA Ops:
  0.6 135.1 %copy-start = (bf16[1,1,1024,768]{3,2,1,0:T(8,128)(2,1)S(1)}, bf16[1,1,1024,768]{3,2,1,0:T(8,128)(2,1)}, u32[]{:S(2)}) copy-start(bf16[1,1,1024,768]{3,2,1,0:T(8,128)(2,1)} %param.17) | copy-start | bytes 4718596
  0.6 4.6 %copy-start.5 = (bf16[1,128,4096]{2,1,0:T(8,128)(2,1)S(1)}, bf16[1,128,4096]{2,1,0:T(8,128)(2,1)}, u32[]{:S(2)}) copy-start(bf16[1,128,4096]{2,1,0:T(8,128)(2,1)} %param.13) | copy-start | bytes 3145732
  2.6 4.2 copy-start.12
  6.9 2.8 copy-start.6
  12.8 2.3 copy-start.4
  18.5 114.4 %all-to-all-start = ((bf16[32,72,1024]{2,1,0:T(8,128)(2,1)}), bf16[32,72,1024]{2,1,0:T(8,128)(2,1)}, u32[]{:S(2)}, u32[]{:S(2)}) async-start(bf16[32,72,1024]{2,1,0:T(8,128)(2,1)} %pad_maximum_fusion), calls=%async_computation | async-start | bytes 9437184 | tf_op jit(solution)/shard_map/all_to_all | solution.py:164
  135.7 1.4 copy-start.10
  138.5 3.0 copy-start.3
  141.6 2.4 copy-start.8
  142.9 14.4 %collective-permute-start = (bf16[2,192,1536]{2,1,0:T(8,128)(2,1)}, bf16[2,192,1536]{2,1,0:T(8,128)(2,1)}, u32[]{:S(2)}, u32[]{:S(2)}) collective-permute-start(bf16[2,192,1536]{2,1,0:T(8,128)(2,1)} %fusion.32), channel_id=1, source_target_pairs={{0,1},{1,0},{2,3},{3,2},{4,5},{5,4},{6,7},{7,6},{8,9},{9,8},{10,11... | collective-permute-start | bytes 3538952 | tf_op jit(solution)/shard_map/ppermute | solution.py:14
  156.8 6.7 %collective-permute-start.4 = (bf16[2,192,2304]{2,1,0:T(8,128)(2,1)}, bf16[2,192,2304]{2,1,0:T(8,128)(2,1)}, u32[]{:S(2)}, u32[]{:S(2)}) collective-permute-start(bf16[2,192,2304]{2,1,0:T(8,128)(2,1)} %select_bitcast_fusion.1), channel_id=1, source_target_pairs={{0,1},{1,0},{2,3},{3,2},{4,5},{5,4},{6,7},{7,6},{8,9},{9,8},{10,11... | collective-permute-start | bytes 5308424 | tf_op jit(solution)/shard_map/ppermute | solution.py:14
  159.4 4.1 copy-start.1
  159.5 93.5 %collective-permute-start.1 = (f32[192,1536]{1,0:T(8,128)S(1)}, f32[192,1536]{1,0:T(8,128)S(1)}, u32[]{:S(2)}, u32[]{:S(2)}) collective-permute-start(f32[192,1536]{1,0:T(8,128)S(1)} %select_bitcast_fusion.2), channel_id=1, source_target_pairs={{0,2},{2,0},{1,3},{3,1},{4,6},{6,4},{5,7},{7,5},{8,10},{10,8},{9,1... | collective-permute-start | bytes 3538952 | tf_op jit(solution)/shard_map/ppermute | solution.py:14
  165.7 131.5 %collective-permute-start.5 = (f32[192,2304]{1,0:T(8,128)S(1)}, f32[192,2304]{1,0:T(8,128)S(1)}, u32[]{:S(2)}, u32[]{:S(2)}) collective-permute-start(f32[192,2304]{1,0:T(8,128)S(1)} %select_bitcast_fusion), channel_id=1, source_target_pairs={{0,2},{2,0},{1,3},{3,1},{4,6},{6,4},{5,7},{7,5},{8,10},{10,8},{9,1... | collective-permute-start | bytes 5308424 | tf_op jit(solution)/shard_map/ppermute | solution.py:14
  253.5 62.8 %collective-permute-start.2 = (bf16[192,768]{1,0:T(8,128)(2,1)S(1)}, bf16[192,768]{1,0:T(8,128)(2,1)S(1)}, u32[]{:S(2)}, u32[]{:S(2)}) collective-permute-start(bf16[192,768]{1,0:T(8,128)(2,1)S(1)} %fusion.46), channel_id=1, source_target_pairs={{0,2},{2,0},{1,3},{3,1},{4,6},{6,4},{5,7},{7,5},{8,10},{10,8},{9,1... | collective-permute-start | bytes 884744 | tf_op jit(solution)/shard_map/ppermute | solution.py:14
  298.0 30.9 %collective-permute-start.6 = (bf16[192,1536]{1,0:T(8,128)(2,1)S(1)}, bf16[192,1536]{1,0:T(8,128)(2,1)S(1)}, u32[]{:S(2)}, u32[]{:S(2)}) collective-permute-start(bf16[192,1536]{1,0:T(8,128)(2,1)S(1)} %get-tuple-element.16), channel_id=1, source_target_pairs={{0,2},{2,0},{1,3},{3,1},{4,6},{6,4},{5,7},{7,5},{8,10},{10,8},{9,1... | collective-permute-start | bytes 1769480 | tf_op jit(solution)/shard_map/ppermute | solution.py:14
  316.3 13.6 %collective-permute-start.3 = (bf16[2,192,768]{2,1,0:T(8,128)(2,1)S(1)}, bf16[2,192,768]{2,1,0:T(8,128)(2,1)S(1)}, u32[]{:S(2)}, u32[]{:S(2)}) collective-permute-start(bf16[2,192,768]{2,1,0:T(8,128)(2,1)S(1)} %get-tuple-element.14), channel_id=1, source_target_pairs={{0,1},{1,0},{2,3},{3,2},{4,5},{5,4},{6,7},{7,6},{8,9},{9,8},{10,11... | collective-permute-start | bytes 1769480 | tf_op jit(solution)/shard_map/ppermute | solution.py:14
  329.0 4.3 collective-permute-start.7
  330.5 1.4 copy-start.9
  334.6 1.4 copy-start.11
  414.8 3.8 copy-start.2
  414.8 3.8 copy-start.7
  416.3 34.9 %collective-permute-start.9 = (bf16[1,128,4096]{2,1,0:T(8,128)(2,1)}, bf16[1,128,4096]{2,1,0:T(8,128)(2,1)}, u32[]{:S(2)}, u32[]{:S(2)}) collective-permute-start(bf16[1,128,4096]{2,1,0:T(8,128)(2,1)} %fusion.1), channel_id=1, source_target_pairs={{32,0},{64,32},{96,64},{128,96},{160,128},{192,160},{224,192},{33,... | collective-permute-start | bytes 3145736 | tf_op jit(solution)/shard_map/ppermute | solution.py:20
  420.4 33.4 %collective-permute-start.8 = (bf16[1,128,4096]{1,2,0:T(8,128)(2,1)}, bf16[1,128,4096]{1,2,0:T(8,128)(2,1)S(1)}, u32[]{:S(2)}, u32[]{:S(2)}) collective-permute-start(bf16[1,128,4096]{1,2,0:T(8,128)(2,1)} %bitcast.195), channel_id=1, source_target_pairs={{0,32},{32,64},{64,96},{96,128},{128,160},{160,192},{192,224},{1,3... | collective-permute-start | bytes 3145736 | tf_op jit(solution)/shard_map/ppermute | solution.py:20

commit v3 on v2

--- a/solution.py
+++ b/solution.py
@@ -1,7 +1,11 @@
+import functools
+
 import jax
 import jax.numpy as jnp
 from jax import lax
 from jax.sharding import PartitionSpec as P
+from jax.experimental import pallas as pl
+from jax.experimental.pallas import tpu as pltpu
 
 
 def partner(block, axis, distance):
@@ -135,6 +139,58 @@
         grads[:, proj_width:], w_up
     )
     return result.astype(jnp.bfloat16)
+
+
+def return_kernel(pp_count, ep_count, step, src_ref, dst_ref, send_sem, recv_sem):
+    stage = lax.axis_index("pp")
+    me = lax.axis_index("ep")
+    sends = (stage + step >= 0) & (stage + step < pp_count)
+    receives = (stage - step >= 0) & (stage - step < pp_count)
+    mesh_ids = pl.DeviceIdType.MESH
+    barrier = pltpu.get_barrier_semaphore()
+
+    def each(body):
+        @pl.loop(0, ep_count)
+        def _(offset):
+            body(lax.rem(me + 1 + offset, ep_count))
+
+    def greet(target):
+        each(lambda n: pl.semaphore_signal(barrier, 1, device_id=(target, n), device_id_type=mesh_ids))
+
+    pl.when(sends)(lambda: greet(stage + step))
+    pl.when(receives)(lambda: greet(stage - step))
+    pl.when(sends & receives)(lambda: pl.semaphore_wait(barrier, 2 * ep_count))
+    pl.when(sends != receives)(lambda: pl.semaphore_wait(barrier, ep_count))
+
+    def copy(n, sender):
+        return pltpu.make_async_remote_copy(
+            src_ref=src_ref.at[n],
+            dst_ref=dst_ref.at[sender],
+            send_sem=send_sem.at[n],
+            recv_sem=recv_sem.at[sender],
+            device_id=(stage + step, n),
+            device_id_type=mesh_ids,
+        )
+
+    pl.when(sends)(lambda: each(lambda n: copy(n, me).start()))
+    pl.when(sends)(lambda: each(lambda n: copy(n, me).wait_send()))
+    pl.when(receives)(lambda: each(lambda j: copy(me, j).wait_recv()))
+
+
+def send_back(out_block, step, kernel_id):
+    pp_count = lax.axis_size("pp")
+    ep_count = lax.axis_size("ep")
+    return pl.pallas_call(
+        functools.partial(return_kernel, pp_count, ep_count, step),
+        out_shape=jax.ShapeDtypeStruct(out_block.shape, out_block.dtype),
+        in_specs=[pl.BlockSpec(memory_space=pl.ANY)],
+        out_specs=pl.BlockSpec(memory_space=pl.ANY),
+        scratch_shapes=[
+            pltpu.SemaphoreType.DMA((ep_count,)),
+            pltpu.SemaphoreType.DMA((ep_count,)),
+        ],
+        compiler_params=pltpu.CompilerParams(collective_id=kernel_id, has_side_effects=True),
+    )(out_block)
 
 
 def on_device(
@@ -160,17 +216,17 @@
     send_rows = device_rows(spread_rows(places_bwd, bwd_tokens[0]))
     slot_gate = jnp.einsum("tkec,tk->ec", places_bwd, bwd_gates[0], precision=lax.Precision.HIGHEST)
     send_grads = device_rows(spread_rows(places_bwd, bwd_grads[0]) * slot_gate[:, None, :, None])
-    slot_cap_fwd = send_fwd.shape[1]
+    recv_fwd = lax.all_to_all(send_fwd, "ep", split_axis=0, concat_axis=0, tiled=True)
+    slot_cap_bwd = send_rows.shape[1]
     received = lax.all_to_all(
-        jnp.concatenate([send_fwd, send_rows, send_grads], axis=1),
+        jnp.concatenate([send_rows, send_grads], axis=1),
         "ep",
         split_axis=0,
         concat_axis=0,
         tiled=True,
     )
-    recv_fwd = received[:, :slot_cap_fwd]
-    recv_rows = received[:, slot_cap_fwd : 2 * slot_cap_fwd]
-    recv_grads = received[:, 2 * slot_cap_fwd :]
+    recv_rows = received[:, :slot_cap_bwd]
+    recv_grads = received[:, slot_cap_bwd:]
     quarter_width = send_fwd.shape[2]
     w_gate = gate_proj[0, 0]
     w_up = up_proj[0, 0]
@@ -185,22 +241,26 @@
         w_up,
         w_down,
     ).reshape(recv_rows.shape)
-    back = lax.all_to_all(
-        jnp.concatenate([out_fwd, out_bwd], axis=1), "ep", split_axis=0, concat_axis=0, tiled=True
-    )
-    back_fwd = back[:, :slot_cap_fwd]
-    back_bwd = back[:, slot_cap_fwd:]
-    gathered = collect(places_fwd, back_fwd)
+    back_fwd = send_back(out_fwd, 1, 0)
+    back_bwd = send_back(out_bwd, -1, 1)
+    stage = lax.axis_index("pp")
+    pp_count = lax.axis_size("pp")
+    routes_prev = shifted(fwd_routes, "pp", 1)
+    gates_prev = shifted(fwd_gates, "pp", 1)
+    routes_next = shifted(bwd_routes, "pp", -1)
+    places_prev = slot_places(routes_prev[0], expert_count, slot_cap)
+    places_next = slot_places(routes_next[0], expert_count, slot_cap)
+    gathered = collect(places_prev, back_fwd)
     mixture = (
-        jnp.sum(gathered * fwd_gates[0][:, :, None, None], axis=1)
+        jnp.sum(gathered * gates_prev[0][:, :, None, None], axis=1)
         .reshape(tok_count, -1)
         .astype(jnp.bfloat16)
     )
     grad_input = (
-        jnp.sum(collect(places_bwd, back_bwd), axis=1).reshape(tok_count, -1).astype(jnp.bfloat16)
-    )
-    handed_forward = shifted(mixture[None], "pp", 1)
-    handed_backward = shifted(grad_input[None], "pp", -1)
+        jnp.sum(collect(places_next, back_bwd), axis=1).reshape(tok_count, -1).astype(jnp.bfloat16)
+    )
+    handed_forward = jnp.where(stage == 0, jnp.zeros_like(mixture), mixture)[None]
+    handed_backward = jnp.where(stage == pp_count - 1, jnp.zeros_like(grad_input), grad_input)[None]
     return (handed_forward, handed_backward)
 
 

time: 464 us -> 459 us (0.989)
  Pallas kernels: 0 us -> 90.8 us
  blocking collectives: 70.1 us -> 0 us
  waiting for transfers between devices: 284 us -> 246 us
  other arithmetic: 19.7 us -> 27.9 us
  matrix products: 19.3 us -> 26.8 us
    pallas_call x0 -> x2, Pallas kernels: none -> 90.8 us  [send_back(): pl.pallas_call(functools.partial(return_kernel, pp_count, ep_count, step)...]
    all_to_all x1 -> x0, blocking collectives: 70.1 us -> none  [on_device(): lax.all_to_all(jnp.concatenate([out_fwd, out_bwd], axis=1), 'ep', split_a...]
    ppermute x2 -> x3, waiting for transfers between devices: 22.4 us -> 0.01 us  [shifted(): return lax.ppermute(shard, axis, pairs)]
    all_to_all x1 -> x2, waiting for transfers between devices: 102 us -> 90.7 us  [the longest x1 64.5 us: on_device(): lax.all_to_all(jnp.concatenate([send_rows, send_grads], axis=1), 'ep', sp...]
    all_to_all x1 -> x2, starting transfers between devices: 12 us -> 21.5 us  [the longest x1 12.1 us: on_device(): lax.all_to_all(send_fwd, 'ep', split_axis=0, concat_axis=0, tiled=True)]
    ppermute x2 -> x3, starting transfers between devices: 13.4 us -> 9.3 us  [shifted(): return lax.ppermute(shard, axis, pairs)]
  transfers between devices with their start and end apart: 11 -> 13, of which waited for: 7 -> 5; matrix products, arithmetic and copies ran while one was open for 5% -> 13% of each run, Pallas kernels for 0% -> 10%
where the time goes in v3:
time: 459 us; the launch traced here: 454 us
  waiting for transfers between devices  246 us (54%)
  Pallas kernels  90.8 us (20%)
  starting transfers between devices  36.4 us (8%)
  other arithmetic  27.9 us (6%)
  matrix products  26.8 us (6%)
  local copies, waits for them, and re-layouts  24.4 us (5%)
    ppermute x8, waiting for transfers between devices, partner(): return lax.ppermute(block, axis, route)  155 us
    pallas_call x2, Pallas kernels, send_back(): pl.pallas_call(functools.partial(return_kernel, pp_count, ep_count, step)...  90.8 us
    all_to_all x1, waiting for transfers between devices, on_device(): lax.all_to_all(jnp.concatenate([send_rows, send_grads], axis=1), 'ep', sp...  64.5 us
    all_to_all x1, waiting for transfers between devices, on_device(): lax.all_to_all(send_fwd, 'ep', split_axis=0, concat_axis=0, tiled=True)  26.1 us
    all_to_all x1, starting transfers between devices, on_device(): lax.all_to_all(send_fwd, 'ep', split_axis=0, concat_axis=0, tiled=True)  12.1 us
    all_to_all x1, starting transfers between devices, on_device(): lax.all_to_all(jnp.concatenate([send_rows, send_grads], axis=1), 'ep', sp...  9.39 us
    ppermute x3, starting transfers between devices, shifted(): return lax.ppermute(shard, axis, pairs)  9.3 us
  transfers between devices with their start and end apart: 13, of which 5 were waited for; matrix products, arithmetic and copies ran while one was open for 13% of the time, Pallas kernels for 10%

profile of v3, /device:TPU:31, one launch (start us, length us, event | category | flops | bytes accessed | tf_op | source)
XLA Modules:
  0.0 453.5 jit_solution(15554954200073413501)
XLA Ops:
  2.6 1.9 reshape_squeeze.9
  4.5 2.1 convolution_convert_fusion.2
  6.6 12.1 %all-to-all-start = ((bf16[32,24,1024]{2,1,0:T(8,128)(2,1)}), bf16[32,24,1024]{2,1,0:T(8,128)(2,1)}, u32[]{:S(2)}, u32[]{:S(2)}) async-start(bf16[32,24,1024]{2,1,0:T(8,128)(2,1)} %bitcast.7), calls=%async_computation | async-start | bytes 3145728 | tf_op jit(solution)/shard_map/all_to_all | solution.py:219
  19.0 1.9 reshape_squeeze.11
  20.9 2.6 reshape_squeeze.10
  24.3 2.2 convolution_convert_fusion
  26.5 1.0 multiply_convert_fusion
  27.5 2.0 pad_maximum_fusion.1
  29.4 26.1 %all-to-all-done = bf16[32,24,1024]{2,1,0:T(8,128)(2,1)} async-done(((bf16[32,24,1024]{2,1,0:T(8,128)(2,1)}), bf16[32,24,1024]{2,1,0:T(8,128)(2,1)}, u32[]{:S(2)}, u32[]{:S(2)}) %all-to-all-start) | async-done | bytes 1572896 | tf_op jit(solution)/shard_map/all_to_all | solution.py:219
  55.6 9.4 %all-to-all-start.1 = ((bf16[32,48,1024]{2,1,0:T(8,128)(2,1)}), bf16[32,48,1024]{2,1,0:T(8,128)(2,1)}, u32[]{:S(2)}, u32[]{:S(2)}) async-start(bf16[32,48,1024]{2,1,0:T(8,128)(2,1)} %pad_maximum_fusion.1), calls=%async_computation.1 | async-start | bytes 6291456 | tf_op jit(solution)/shard_map/all_to_all | solution.py:221
  65.0 2.9 fusion.27
  68.0 2.8 fusion.30
  70.8 1.5 fusion.33
  72.6 64.5 %all-to-all-done.1 = bf16[32,48,1024]{2,1,0:T(8,128)(2,1)} async-done(((bf16[32,48,1024]{2,1,0:T(8,128)(2,1)}), bf16[32,48,1024]{2,1,0:T(8,128)(2,1)}, u32[]{:S(2)}, u32[]{:S(2)}) %all-to-all-start.1) | async-done | bytes 3145760 | tf_op jit(solution)/shard_map/all_to_all | solution.py:221
  137.1 2.2 fusion.89
  139.3 1.5 fusion.18
  140.8 1.5 fusion.21
  142.3 1.4 fusion.24
  143.8 2.1 pad_maximum_fusion
  145.9 5.8 %copy.39 = bf16[768,2304]{1,0:T(8,128)(2,1)} copy(bf16[768,2304]{0,1:T(8,128)(2,1)} %pad_maximum_fusion) | data formatting | bytes 7077888 | tf_op jit(solution)/shard_map/concatenate | solution.py:128
  151.7 3.5 select_bitcast_fusion.1
  155.4 2.4 collective-permute-start.6
  157.8 5.0 %collective-permute-start = (s32[1,128,1]{1,2,0:T(1,128)S(1)}, s32[1,128,1]{1,2,0:T(1,128)S(1)}, u32[]{:S(2)}, u32[]{:S(2)}) collective-permute-start(s32[1,128,1]{1,2,0:T(1,128)S(1)} %copy-done.6), channel_id=1, source_target_pairs={{0,32},{32,64},{64,96},{96,128},{128,160},{160,192},{192,224},{1,3... | collective-permute-start | bytes 1544 | tf_op jit(solution)/shard_map/ppermute | solution.py:24
  162.8 1.9 collective-permute-start.5
  164.8 2.0 convert_add_fusion.1
  167.0 1.3 copy-done.3
  168.3 2.3 collective-permute-start.2
  170.5 2.0 convert_add_fusion
  172.6 1.6 select_bitcast_fusion
  175.0 1.4 collective-permute-start.8
  177.1 79.3 %collective-permute-done.2 = f32[192,1536]{1,0:T(8,128)} collective-permute-done((f32[192,1536]{1,0:T(8,128)S(1)}, f32[192,1536]{1,0:T(8,128)}, u32[]{:S(2)}, u32[]{:S(2)}) %collective-permute-start.2) | collective-permute-done | bytes 1179680 | tf_op jit(solution)/shard_map/ppermute | solution.py:18
  256.4 2.2 bitcast_add_fusion.1
  259.4 47.4 %collective-permute-done.3 = bf16[192,768]{1,0:T(8,128)(2,1)S(1)} collective-permute-done((bf16[192,768]{1,0:T(8,128)(2,1)S(1)}, bf16[192,768]{1,0:T(8,128)(2,1)S(1)}, u32[]{:S(2)}, u32[]{:S(2)}) %collective-permute-start.3) | collective-permute-done | bytes 294944 | tf_op jit(solution)/shard_map/ppermute | solution.py:18
  307.5 2.8 bitcast_add_fusion
  311.0 28.6 %collective-permute-done.9 = bf16[192,1536]{1,0:T(8,128)(2,1)S(1)} collective-permute-done((bf16[192,1536]{1,0:T(8,128)(2,1)S(1)}, bf16[192,1536]{1,0:T(8,128)(2,1)S(1)}, u32[]{:S(2)}, u32[]{:S(2)}) %collective-permute-start.9) | collective-permute-done | bytes 589856 | tf_op jit(solution)/shard_map/ppermute | solution.py:18
  339.6 1.2 fusion.88
  341.8 1.3 copy-done.8
  343.1 2.5 convolution_convert_fusion.1
  345.7 45.3 %shard_map.113 = bf16[32,24,1024]{2,1,0:T(8,128)(2,1)} custom-call(bf16[32,24,1024]{2,1,0:T(8,128)(2,1)} %bitcast.196), custom_call_target="tpu_custom_call" | custom-call | tf_op jit(solution)/shard_map/pallas_call | solution.py:183
  390.9 2.8 fusion.38
  393.8 2.3 copy.34
  396.1 2.3 copy.44
  398.3 1.5 pad_maximum_fusion.2
  400.9 1.4 fusion.16
  402.4 2.6 add_convert_fusion
  404.9 45.6 %shard_map.114 = bf16[32,24,1024]{2,1,0:T(8,128)(2,1)} custom-call(bf16[32,24,1024]{2,1,0:T(8,128)(2,1)} %bitcast.195), custom_call_target="tpu_custom_call" | custom-call | tf_op jit(solution)/shard_map/pallas_call | solution.py:183
  450.5 1.6 copy.54
  452.1 1.4 fusion.2
  (72 shorter events, 9.5 us)
Async XLA Ops:
  0.6 64.4 %copy-start = (bf16[1,1,1024,768]{3,2,1,0:T(8,128)(2,1)S(1)}, bf16[1,1,1024,768]{3,2,1,0:T(8,128)(2,1)}, u32[]{:S(2)}) copy-start(bf16[1,1,1024,768]{3,2,1,0:T(8,128)(2,1)} %param.17) | copy-start | bytes 4718596
  6.6 12.1 %copy-start.5 = (s32[1,128,1]{1,2,0:T(1,128)S(1)}, s32[1,128,1]{1,2,0:T(1,128)}, u32[]{:S(2)}) copy-start(s32[1,128,1]{1,2,0:T(1,128)} %param.15) | copy-start | bytes 1540
  6.6 49.0 %all-to-all-start = ((bf16[32,24,1024]{2,1,0:T(8,128)(2,1)}), bf16[32,24,1024]{2,1,0:T(8,128)(2,1)}, u32[]{:S(2)}, u32[]{:S(2)}) async-start(bf16[32,24,1024]{2,1,0:T(8,128)(2,1)} %bitcast.7), calls=%async_computation | async-start | bytes 3145728 | tf_op jit(solution)/shard_map/all_to_all | solution.py:219
  20.9 2.8 copy-start.12
  55.6 81.5 %all-to-all-start.1 = ((bf16[32,48,1024]{2,1,0:T(8,128)(2,1)}), bf16[32,48,1024]{2,1,0:T(8,128)(2,1)}, u32[]{:S(2)}, u32[]{:S(2)}) async-start(bf16[32,48,1024]{2,1,0:T(8,128)(2,1)} %pad_maximum_fusion.1), calls=%async_computation.1 | async-start | bytes 6291456 | tf_op jit(solution)/shard_map/all_to_all | solution.py:221
  65.0 2.9 copy-start.9
  70.8 1.5 copy-start.4
  72.2 92.5 %collective-permute-start.1 = (bf16[2,192,1536]{2,1,0:T(8,128)(2,1)}, bf16[2,192,1536]{2,1,0:T(8,128)(2,1)}, u32[]{:S(2)}, u32[]{:S(2)}) collective-permute-start(bf16[2,192,1536]{2,1,0:T(8,128)(2,1)} %fusion.33), channel_id=1, source_target_pairs={{0,1},{1,0},{2,3},{3,2},{4,5},{5,4},{6,7},{7,6},{8,9},{9,8},{10,11... | collective-permute-start | bytes 3538952 | tf_op jit(solution)/shard_map/ppermute | solution.py:18
  139.3 1.5 copy-start.10
  140.8 1.5 copy-start.7
  151.7 6.1 %copy-start.6 = (s32[1,128,1]{1,2,0:T(1,128)S(1)}, s32[1,128,1]{1,2,0:T(1,128)}, u32[]{:S(2)}) copy-start(s32[1,128,1]{1,2,0:T(1,128)} %param.11) | copy-start | bytes 1540
  155.1 15.4 %collective-permute-start.7 = (bf16[2,192,2304]{2,1,0:T(8,128)(2,1)}, bf16[2,192,2304]{2,1,0:T(8,128)(2,1)}, u32[]{:S(2)}, u32[]{:S(2)}) collective-permute-start(bf16[2,192,2304]{2,1,0:T(8,128)(2,1)} %select_bitcast_fusion.1), channel_id=1, source_target_pairs={{0,1},{1,0},{2,3},{3,2},{4,5},{5,4},{6,7},{7,6},{8,9},{9,8},{10,11... | collective-permute-start | bytes 5308424 | tf_op jit(solution)/shard_map/ppermute | solution.py:18
  155.4 21.0 %collective-permute-start.6 = (s32[1,128,1]{1,2,0:T(1,128)S(1)}, s32[1,128,1]{1,2,0:T(1,128)S(1)}, u32[]{:S(2)}, u32[]{:S(2)}) collective-permute-start(s32[1,128,1]{1,2,0:T(1,128)S(1)} %copy-done.5), channel_id=1, source_target_pairs={{32,0},{64,32},{96,64},{128,96},{160,128},{192,160},{224,192},{33,... | collective-permute-start | bytes 1544 | tf_op jit(solution)/shard_map/ppermute | solution.py:24
  157.8 18.9 %collective-permute-start = (s32[1,128,1]{1,2,0:T(1,128)S(1)}, s32[1,128,1]{1,2,0:T(1,128)S(1)}, u32[]{:S(2)}, u32[]{:S(2)}) collective-permute-start(s32[1,128,1]{1,2,0:T(1,128)S(1)} %copy-done.6), channel_id=1, source_target_pairs={{0,32},{32,64},{64,96},{96,128},{128,160},{160,192},{192,224},{1,3... | collective-permute-start | bytes 1544 | tf_op jit(solution)/shard_map/ppermute | solution.py:24
  162.8 228.1 %collective-permute-start.5 = (f32[1,128,1]{1,2,0:T(1,128)}, f32[1,128,1]{1,2,0:T(1,128)S(1)}, u32[]{:S(2)}, u32[]{:S(2)}) collective-permute-start(f32[1,128,1]{1,2,0:T(1,128)} %param.12), channel_id=1, source_target_pairs={{0,32},{32,64},{64,96},{96,128},{128,160},{160,192},{192,224},{1,3... | collective-permute-start | bytes 1544 | tf_op jit(solution)/shard_map/ppermute | solution.py:24
  166.8 1.4 copy-start.3
  166.8 3.7 copy-start.1
  168.3 88.1 %collective-permute-start.2 = (f32[192,1536]{1,0:T(8,128)S(1)}, f32[192,1536]{1,0:T(8,128)}, u32[]{:S(2)}, u32[]{:S(2)}) collective-permute-start(f32[192,1536]{1,0:T(8,128)S(1)} %select_bitcast_fusion.2), channel_id=1, source_target_pairs={{0,2},{2,0},{1,3},{3,1},{4,6},{6,4},{5,7},{7,5},{8,10},{10,8},{9,1... | collective-permute-start | bytes 3538952 | tf_op jit(solution)/shard_map/ppermute | solution.py:18
  172.6 2.4 copy-start.2
  175.0 132.5 %collective-permute-start.8 = (f32[192,2304]{1,0:T(8,128)}, f32[192,2304]{1,0:T(8,128)}, u32[]{:S(2)}, u32[]{:S(2)}) collective-permute-start(f32[192,2304]{1,0:T(8,128)} %select_bitcast_fusion), channel_id=1, source_target_pairs={{0,2},{2,0},{1,3},{3,1},{4,6},{6,4},{5,7},{7,5},{8,10},{10,8},{9,1... | collective-permute-start | bytes 5308424 | tf_op jit(solution)/shard_map/ppermute | solution.py:18
  258.8 48.0 %collective-permute-start.3 = (bf16[192,768]{1,0:T(8,128)(2,1)S(1)}, bf16[192,768]{1,0:T(8,128)(2,1)S(1)}, u32[]{:S(2)}, u32[]{:S(2)}) collective-permute-start(bf16[192,768]{1,0:T(8,128)(2,1)S(1)} %fusion.48), channel_id=1, source_target_pairs={{0,2},{2,0},{1,3},{3,1},{4,6},{6,4},{5,7},{7,5},{8,10},{10,8},{9,1... | collective-permute-start | bytes 884744 | tf_op jit(solution)/shard_map/ppermute | solution.py:18
  306.9 3.9 collective-permute-start.4
  310.7 28.9 %collective-permute-start.9 = (bf16[192,1536]{1,0:T(8,128)(2,1)S(1)}, bf16[192,1536]{1,0:T(8,128)(2,1)S(1)}, u32[]{:S(2)}, u32[]{:S(2)}) collective-permute-start(bf16[192,1536]{1,0:T(8,128)(2,1)S(1)} %get-tuple-element.11), channel_id=1, source_target_pairs={{0,2},{2,0},{1,3},{3,1},{4,6},{6,4},{5,7},{7,5},{8,10},{10,8},{9,1... | collective-permute-start | bytes 1769480 | tf_op jit(solution)/shard_map/ppermute | solution.py:18
  340.8 57.5 %collective-permute-start.10 = (bf16[2,192,1536]{2,1,0:T(8,128)(2,1)}, bf16[2,192,1536]{2,1,0:T(8,128)(2,1)}, u32[]{:S(2)}, u32[]{:S(2)}) collective-permute-start(bf16[2,192,1536]{2,1,0:T(8,128)(2,1)} %get-tuple-element.9), channel_id=1, source_target_pairs={{0,1},{1,0},{2,3},{3,2},{4,5},{5,4},{6,7},{7,6},{8,9},{9,8},{10,11... | collective-permute-start | bytes 3538952 | tf_op jit(solution)/shard_map/ppermute | solution.py:18
  341.7 1.4 copy-start.8
  400.9 1.4 copy-start.11
